TPU v7x, 256 devices: a whole 4x4x8 slice. The times are simulated.
256 devices in a mesh: dp: 16 (over z_lo, x), tensor: 16 (over y, z_hi, core).
Axes of the slice: x: 4, y: 4, z: 8 (z_hi: 2, z_lo: 4; z = z_hi * 4 + z_lo), core: 2. Of those that a mesh axis runs over, the one named last changes fastest.
Arguments:
- out_grad: bfloat16 [2048, 5120], P('dp'), may hold values from -6 to 6
- gate_act: bfloat16 [2048, 25600], P('dp', 'tensor'), may hold values from -6 to 6
- up_act: bfloat16 [2048, 25600], P('dp', 'tensor'), may hold values from -6 to 6
- codes: int32 [5120, 25600], P('dp', 'tensor'), may hold values from 0 to 15
- zero_points: int32 [5120, 400], P('dp', 'tensor'), may hold values from 0 to 15
- scales: float32 [5120, 400], P('dp', 'tensor'), may hold values from 0.0009782797 to 0.003913119
- rotation: bfloat16 [1600, 1600], replicated, may hold values from -0.15625 to 0.15625
Outputs:
- grad_gate: bfloat16 [2048, 25600], P('dp', 'tensor')
- grad_up: bfloat16 [2048, 25600], P('dp', 'tensor')
- log_scale_grad: float32 [5120, 400], P('dp', 'tensor')
All inputs are finite; a program needn't handle non-finite values.
Results may differ from a plain program's by a relative error of at most 0.011.
Values may be sent and summed in bfloat16 or wider, within the bound.
A program may use at most 128 MiB of HBM per device.

v0:
```python
import math
import jax
import jax.numpy as jnp
from jax import lax
from jax.sharding import PartitionSpec as P


def sylvester(order_size):
    indices = jnp.arange(order_size, dtype=jnp.int32)
    common_bits = indices[:, None] & indices[None, :]
    parity = jnp.zeros((order_size, order_size), jnp.int32)
    for bit_number in range(order_size.bit_length()):
        parity = parity + (common_bits >> bit_number & 1)
    return (1 - 2 * (parity % 2)).astype(jnp.float32)


def spread(blocks, block_size):
    tok_rows = blocks.shape[0]
    local_blocks = blocks.shape[1] // block_size
    devices = lax.axis_size("tensor")
    norm_factor = 1.0 / math.sqrt(devices * local_blocks)
    hadamard = sylvester(devices * local_blocks).reshape(
        devices, local_blocks, devices, local_blocks
    )
    stacked = blocks.reshape(1, tok_rows, local_blocks, block_size)
    summed = jnp.einsum(
        "qtjc,qjpk->ptkc",
        lax.all_to_all(stacked, "tensor", split_axis=3, concat_axis=0, tiled=True).astype(
            jnp.float32
        ),
        hadamard,
        precision=lax.Precision.HIGHEST,
    )
    summed = (summed * norm_factor).astype(jnp.bfloat16)
    result = lax.all_to_all(summed, "tensor", split_axis=0, concat_axis=3, tiled=True)
    return result.reshape(tok_rows, local_blocks * block_size)


def on_device(out_grad, gate_act, up_act, codes, zero_points, scales, rotation):
    columns = gate_act.shape[1]
    block_size = rotation.shape[0]
    feat_rows = codes.shape[0]
    groups_here = scales.shape[1]
    group_cols = columns // groups_here
    gate32 = gate_act.astype(jnp.float32)
    up32 = up_act.astype(jnp.float32)
    sigmoid_gate = jax.nn.sigmoid(gate32)
    hidden = (gate32 * sigmoid_gate * up32).astype(jnp.bfloat16)
    mixed = jnp.dot(hidden, rotation, preferred_element_type=jnp.float32)
    mixed = mixed.astype(jnp.bfloat16)
    rotated = spread(mixed, block_size)
    levels = (codes.reshape(feat_rows, groups_here, group_cols) - zero_points[:, :, None]).astype(
        jnp.float32
    )
    weight = (levels * scales[:, :, None]).astype(jnp.bfloat16).reshape(feat_rows, columns)
    grad_slice = lax.all_to_all(out_grad, "dp", split_axis=1, concat_axis=0, tiled=True)
    weight_grad = lax.dot_general(
        grad_slice,
        lax.all_gather(rotated, "dp", axis=0, tiled=True),
        (((0,), (0,)), ((), ())),
        preferred_element_type=jnp.float32,
    )
    log_scale_grad = (
        jnp.sum(weight_grad.reshape(feat_rows, groups_here, group_cols) * levels, axis=2) * scales
    )
    grad_rotated = lax.psum_scatter(
        jnp.dot(grad_slice, weight, preferred_element_type=jnp.float32),
        "dp",
        scatter_dimension=0,
        tiled=True,
    )
    grad_mixed = spread(grad_rotated.astype(jnp.bfloat16), block_size)
    grad_hidden = lax.dot_general(
        grad_mixed, rotation, (((1,), (1,)), ((), ())), preferred_element_type=jnp.float32
    )
    grad_gate = (grad_hidden * up32 * sigmoid_gate * (1.0 + gate32 * (1.0 - sigmoid_gate))).astype(
        jnp.bfloat16
    )
    grad_up = (grad_hidden * gate32 * sigmoid_gate).astype(jnp.bfloat16)
    return (grad_gate, grad_up, log_scale_grad)


def solution(mesh):
    return jax.shard_map(
        on_device,
        mesh=mesh,
        in_specs=(
            P("dp", None),
            P("dp", "tensor"),
            P("dp", "tensor"),
            P("dp", "tensor"),
            P("dp", "tensor"),
            P("dp", "tensor"),
            P(),
        ),
        out_specs=(P("dp", "tensor"), P("dp", "tensor"), P("dp", "tensor")),
        check_vma=False,
    )
```

profile of v0, /device:TPU:90, one launch (start us, length us, event | category | flops | bytes accessed | tf_op | source)
XLA Modules:
  0.0 396.5 jit_solution(10725968039748546528)
XLA Ops:
  7.2 2.4 copy.24
  9.6 8.0 %all-to-all-start = ((bf16[128,16,320]{0,2,1:T(8,128)(2,1)}), bf16[128,16,320]{0,2,1:T(8,128)(2,1)}, u32[]{:S(2)}, u32[]{:S(2)}) async-start(bf16[128,16,320]{0,2,1:T(8,128)(2,1)} %bitcast.4), calls=%async_computation | async-start | bytes 2621440 | tf_op jit(solution)/shard_map/all_to_all | solution.py:56
  17.7 2.4 copy.23
  21.4 26.8 %all-to-all-done = bf16[128,16,320]{0,2,1:T(8,128)(2,1)} async-done(((bf16[128,16,320]{0,2,1:T(8,128)(2,1)}), bf16[128,16,320]{0,2,1:T(8,128)(2,1)}, u32[]{:S(2)}, u32[]{:S(2)}) %all-to-all-start) | async-done | bytes 1310752 | tf_op jit(solution)/shard_map/all_to_all | solution.py:56
  48.2 9.9 %convolution_bitcast_fusion = f32[2048,1600]{0,1:T(8,128)} fusion(bf16[320,1600]{0,1:T(8,128)(2,1)} %fusion, bf16[128,16,320]{0,2,1:T(8,128)(2,1)} %all-to-all-done), kind=kOutput, calls=%fused_computation | convolution fusion | flops 2097152000 | bytes 15441920 | tf_op jit(solution)/shard_map/dot_general | solution.py:67
  59.2 4.7 %fusion.2 = bf16[1,128,1,1600]{1,3,2,0:T(8,128)(2,1)S(1)} fusion(bf16[1600,1600]{1,0:T(8,128)(2,1)} %param.13, bf16[128,1600]{0,1:T(8,128)(2,1)S(1)} %copy-done.3, bf16[128,1600]{0,1:T(8,128)(2,1)S(1)} %copy-done.2), kind=kOutput, calls=%fused_computation.8 | convolution fusion | flops 657203200 | bytes 6348800 | tf_op jit(solution)/shard_map/dot_general | solution.py:49
  63.9 6.4 %copy.55 = bf16[1,128,1,1600]{1,2,0,3:T(2,128)(2,1)S(1)} copy(bf16[1,128,1,1600]{1,3,2,0:T(8,128)(2,1)S(1)} %fusion.2) | data formatting | bytes 819200 | tf_op jit(solution)/shard_map/reshape | solution.py:25
  70.8 9.9 %reduce.5 = bf16[1600,128]{1,0:T(8,128)(2,1)} reduce(bf16[1600,1,1,128]{3,2,1,0:T(2,128)(2,1)S(1)} %bitcast.84, bf16[]{:T(256)} %broadcast.409), dimensions={1,2}, to_apply=%bitcast.80.reduce_sub_computation | reduce | bytes 819202
  81.8 21.4 %all_to_all.79 = bf16[16,2,6400]{2,1,0:T(2,128)(2,1)} all-to-all(bf16[16,2,6400]{2,1,0:T(2,128)(2,1)S(1)} %reshape.191), channel_id=1, replica_groups=mesh['dp'=16,'tensor'=16] {'tensor'}, dimensions={0} | all-to-all | bytes 819200 | tf_op jit(solution)/shard_map/all_to_all | solution.py:28
  103.2 2.7 reshape.192
  106.0 7.6 %bitcast_reduce_fusion = bf16[128,1600]{0,1:T(8,128)(2,1)} fusion(bf16[1600,1,1,128]{3,2,1,0:T(2,128)(2,1)S(1)} %reshape.192), kind=kLoop, calls=%fused_computation.60 | loop fusion | bytes 819200 | tf_op jit(solution)/shard_map/all_to_all | solution.py:28
  115.3 18.8 %all_to_all.80 = bf16[16,128,1,100]{1,3,2,0:T(8,128)(2,1)S(1)} all-to-all(bf16[16,128,1,100]{1,3,2,0:T(8,128)(2,1)S(1)} %copy.31), channel_id=1, replica_groups=mesh['dp'=16,'tensor'=16] {'tensor'}, dimensions={0} | all-to-all | bytes 819200 | tf_op jit(solution)/shard_map/all_to_all | solution.py:35
  134.9 83.6 %reduce-scatter.2.cloned.1.call-done = f32[128,1600]{0,1:T(8,128)} async-done(((f32[2048,1600]{0,1:T(8,128)}), f32[128,1600]{0,1:T(8,128)}) %reduce-scatter.2.cloned.1.call-update) | async-done | bytes 819216 | tf_op jit(solution)/shard_map/reduce_scatter | solution.py:66
  219.8 6.4 %copy.56 = bf16[1,128,1,1600]{1,2,0,3:T(2,128)(2,1)S(1)} copy(bf16[1,128,1,1600]{1,3,2,0:T(8,128)(2,1)S(1)} %convert_bitcast_fusion) | data formatting | bytes 819200 | tf_op jit(solution)/shard_map/reshape | solution.py:25
  226.1 9.9 %reduce.4 = bf16[1600,128]{1,0:T(8,128)(2,1)} reduce(bf16[1600,1,1,128]{3,2,1,0:T(2,128)(2,1)S(1)} %bitcast.85, bf16[]{:T(256)} %broadcast.409), dimensions={1,2}, to_apply=%bitcast.81.reduce_sub_computation | reduce | bytes 819202
  237.1 20.5 %all_to_all.81 = bf16[16,2,6400]{2,1,0:T(2,128)(2,1)} all-to-all(bf16[16,2,6400]{2,1,0:T(2,128)(2,1)S(1)} %reshape.189), channel_id=1, replica_groups=mesh['dp'=16,'tensor'=16] {'tensor'}, dimensions={0} | all-to-all | bytes 819200 | tf_op jit(solution)/shard_map/all_to_all | solution.py:28
  257.7 2.7 reshape.190
  260.4 7.6 %bitcast_reduce_fusion.1 = bf16[128,1600]{0,1:T(8,128)(2,1)} fusion(bf16[1600,1,1,128]{3,2,1,0:T(2,128)(2,1)S(1)} %reshape.190), kind=kLoop, calls=%fused_computation.61 | loop fusion | bytes 819200 | tf_op jit(solution)/shard_map/all_to_all | solution.py:28
  270.5 5.8 %all-to-all-start.2 = ((bf16[16,128,1,100]{1,3,2,0:T(8,128)(2,1)}), bf16[16,128,1,100]{1,3,2,0:T(8,128)(2,1)S(1)}, u32[]{:S(2)}, u32[]{:S(2)}) async-start(bf16[16,128,1,100]{1,3,2,0:T(8,128)(2,1)} %copy.28), calls=%async_computation.3 | async-start | bytes 851968 | tf_op jit(solution)/shard_map/all_to_all | solution.py:35
  276.3 94.5 %all-gather.2.cloned.1.call-done = bf16[2048,1600]{0,1:T(8,128)(2,1)} async-done(((bf16[128,1600]{0,1:T(8,128)(2,1)}), bf16[2048,1600]{0,1:T(8,128)(2,1)}) %all-gather.2.cloned.1.call-update) | async-done | bytes 6553616 | tf_op jit(solution)/shard_map/all_gather | solution.py:59
  370.8 7.1 %convolution_bitcast_fusion.1 = f32[320,1600]{1,0:T(8,128)} fusion(bf16[2048,1600]{0,1:T(8,128)(2,1)} %all-gather.2.cloned.1.call-done, bf16[128,16,320]{0,2,1:T(8,128)(2,1)} %all-to-all-done), kind=kOutput, calls=%fused_computation.1 | convolution fusion | flops 2097152000 | bytes 9912320 | tf_op jit(solution)/shard_map/dot_general | solution.py:57
  377.9 3.1 copy.32
  381.0 2.3 multiply_reduce_fusion
  384.0 5.3 %fusion.20 = (bf16[128,1600]{0,1:T(8,128)(2,1)}, bf16[128,1600]{0,1:T(8,128)(2,1)}) fusion(bf16[128,1600]{0,1:T(8,128)(2,1)} %param.8, bf16[128,1600]{0,1:T(8,128)(2,1)} %param.9, bf16[1600,1600]{1,0:T(8,128)(2,1)} %param.13, bf16[128,1600]{0,1:T(8,128)(2,1)S(1)} %reshape.180), kind=kOutput, calls=%fused_computation.34 | convolution fusion | flops 658432000 | bytes 7168000 | tf_op jit(solution)/shard_map/dot_general | solution.py:73
  (27 shorter events, 12.1 us)
Async XLA Ops:
  9.6 38.6 %all-to-all-start = ((bf16[128,16,320]{0,2,1:T(8,128)(2,1)}), bf16[128,16,320]{0,2,1:T(8,128)(2,1)}, u32[]{:S(2)}, u32[]{:S(2)}) async-start(bf16[128,16,320]{0,2,1:T(8,128)(2,1)} %bitcast.4), calls=%async_computation | async-start | bytes 2621440 | tf_op jit(solution)/shard_map/all_to_all | solution.py:56
  17.6 2.4 copy-start
  17.6 2.4 copy-start.1
  17.6 200.9 %reduce-scatter.2.cloned.1.call-start = ((), (), s32[]{:S(2)}) async-start(), calls=%async_computation.6 | async-start | bytes 13926400 | tf_op jit(solution)/shard_map/reduce_scatter | solution.py:66
  58.1 1.0 copy-start.2
  58.1 1.1 copy-start.3
  58.1 312.7 %all-gather.2.cloned.1.call-start = ((), (), s32[]{:S(2)}) async-start(), calls=%async_computation.7 | async-start | bytes 6963200 | tf_op jit(solution)/shard_map/all_gather | solution.py:59
  270.5 113.5 %all-to-all-start.2 = ((bf16[16,128,1,100]{1,3,2,0:T(8,128)(2,1)}), bf16[16,128,1,100]{1,3,2,0:T(8,128)(2,1)S(1)}, u32[]{:S(2)}, u32[]{:S(2)}) async-start(bf16[16,128,1,100]{1,3,2,0:T(8,128)(2,1)} %copy.28), calls=%async_computation.3 | async-start | bytes 851968 | tf_op jit(solution)/shard_map/all_to_all | solution.py:35
Sparse Core Ops, SparseCore 0:
  58.3 160.2 reduce-scatter.1
  220.9 149.8 all-gather.1
where the time goes:
time: 401 us; the launch traced here: 396 us
  waiting for transfers between devices  205 us (51%)
  blocking collectives  60.8 us (15%)
  local copies, waits for them, and re-layouts  48.7 us (12%)
  matrix products  28 us (7%)
  other arithmetic  25.3 us (6%)
  starting transfers between devices  14.4 us (4%)
  between operations  14.4 us (4%)
    all_gather x1, waiting for transfers between devices, on_device(): lax.all_gather(rotated, 'dp', axis=0, tiled=True)  94.5 us
    reduce_scatter x1, waiting for transfers between devices, on_device(): lax.psum_scatter(jnp.dot(grad_slice, weight, preferred_element_type=jnp.f...  83.6 us
    all_to_all x2, blocking collectives, spread(): lax.all_to_all(stacked, 'tensor', split_axis=3, concat_axis=0, tiled=True)  41.9 us
    all_to_all x1, waiting for transfers between devices, on_device(): lax.all_to_all(out_grad, 'dp', split_axis=1, concat_axis=0, tiled=True)  26.8 us
    unnamed x2, other arithmetic  19.8 us
    all_to_all x1, blocking collectives, spread(): lax.all_to_all(summed, 'tensor', split_axis=0, concat_axis=3, tiled=True)  18.8 us
    all_to_all x4, local copies, waits for them, and re-layouts, spread(): lax.all_to_all(stacked, 'tensor', split_axis=3, concat_axis=0, tiled=True)  17.3 us
    unnamed x15, local copies, waits for them, and re-layouts  13.6 us
  transfers between devices with their start and end apart: 4, of which 3 were waited for; matrix products, arithmetic and copies ran while one was open for 21% of the time, Pallas kernels for 0%

commit v1 on v0

--- a/solution.py
+++ b/solution.py
@@ -56,7 +56,9 @@
     grad_slice = lax.all_to_all(out_grad, "dp", split_axis=1, concat_axis=0, tiled=True)
     weight_grad = lax.dot_general(
         grad_slice,
-        lax.all_gather(rotated, "dp", axis=0, tiled=True),
+        jnp.concatenate(
+            lax.all_to_all(jnp.stack([rotated] * lax.axis_size("dp")), "dp", 0, 0), axis=0
+        ),
         (((0,), (0,)), ((), ())),
         preferred_element_type=jnp.float32,
     )

time: 401 us -> 479 us (1.19)
  the two profiles are of different devices: /device:TPU:90 before, /device:TPU:193 now
where the time goes in v1:
time: 479 us; the launch traced here: 470 us
  waiting for transfers between devices  170 us (35%)
  blocking collectives  136 us (28%)
  local copies, waits for them, and re-layouts  54.9 us (11%)
  starting transfers between devices  41 us (9%)
  matrix products  28.1 us (6%)
  other arithmetic  25.7 us (5%)
  between operations  14.4 us (3%)
    all_to_all x1, blocking collectives, spread(): lax.all_to_all(stacked, 'tensor', split_axis=3, concat_axis=0, tiled=True)  136 us
    all_to_all x1, waiting for transfers between devices, on_device(): lax.all_to_all(jnp.stack([rotated] * lax.axis_size('dp')), 'dp', 0, 0)  135 us
    all_to_all x1, waiting for transfers between devices, on_device(): lax.all_to_all(out_grad, 'dp', split_axis=1, concat_axis=0, tiled=True)  27.2 us
    unnamed x2, other arithmetic  20.3 us
    all_to_all x2, starting transfers between devices, spread(): lax.all_to_all(summed, 'tensor', split_axis=0, concat_axis=3, tiled=True)  19.5 us
    all_to_all x4, local copies, waits for them, and re-layouts, spread(): lax.all_to_all(stacked, 'tensor', split_axis=3, concat_axis=0, tiled=True)  17.3 us
    unnamed x17, local copies, waits for them, and re-layouts  14.9 us
    reshape x2, local copies, waits for them, and re-layouts, spread(): stacked = blocks.reshape(1, tok_rows, local_blocks, block_size)  12.7 us
  transfers between devices with their start and end apart: 6, of which 3 were waited for; matrix products, arithmetic and copies ran while one was open for 18% of the time, Pallas kernels for 0%

profile of v1, /device:TPU:193, one launch (start us, length us, event | category | flops | bytes accessed | tf_op | source)
XLA Modules:
  0.0 470.3 jit_solution(4171967760841722243)
XLA Ops:
  7.2 2.4 copy.25
  9.6 6.6 %all-to-all-start = ((bf16[128,16,320]{0,2,1:T(8,128)(2,1)}), bf16[128,16,320]{0,2,1:T(8,128)(2,1)}, u32[]{:S(2)}, u32[]{:S(2)}) async-start(bf16[128,16,320]{0,2,1:T(8,128)(2,1)} %bitcast.4), calls=%async_computation | async-start | bytes 2621440 | tf_op jit(solution)/shard_map/all_to_all | solution.py:56
  20.0 27.2 %all-to-all-done = bf16[128,16,320]{0,2,1:T(8,128)(2,1)} async-done(((bf16[128,16,320]{0,2,1:T(8,128)(2,1)}), bf16[128,16,320]{0,2,1:T(8,128)(2,1)}, u32[]{:S(2)}, u32[]{:S(2)}) %all-to-all-start) | async-done | bytes 1310752 | tf_op jit(solution)/shard_map/all_to_all | solution.py:56
  47.2 9.9 %convolution_bitcast_fusion = f32[2048,1600]{0,1:T(8,128)} fusion(bf16[320,1600]{0,1:T(8,128)(2,1)} %fusion, bf16[128,16,320]{0,2,1:T(8,128)(2,1)} %all-to-all-done), kind=kOutput, calls=%fused_computation | convolution fusion | flops 2097152000 | bytes 15441920 | tf_op jit(solution)/shard_map/dot_general | solution.py:69
  58.2 4.7 %fusion.2 = bf16[1,128,1,1600]{1,3,2,0:T(8,128)(2,1)S(1)} fusion(bf16[1600,1600]{1,0:T(8,128)(2,1)} %param.13, bf16[128,1600]{0,1:T(8,128)(2,1)S(1)} %copy-done.4, bf16[128,1600]{0,1:T(8,128)(2,1)S(1)} %copy-done.3), kind=kOutput, calls=%fused_computation.8 | convolution fusion | flops 657203200 | bytes 6348800 | tf_op jit(solution)/shard_map/dot_general | solution.py:49
  62.9 6.4 %copy.52 = bf16[1,128,1,1600]{1,2,0,3:T(2,128)(2,1)S(1)} copy(bf16[1,128,1,1600]{1,3,2,0:T(8,128)(2,1)S(1)} %fusion.2) | data formatting | bytes 819200 | tf_op jit(solution)/shard_map/reshape | solution.py:25
  69.8 10.4 %reduce.5 = bf16[1600,128]{1,0:T(8,128)(2,1)} reduce(bf16[1600,1,1,128]{3,2,1,0:T(2,128)(2,1)S(1)} %bitcast.83, bf16[]{:T(256)} %broadcast.410), dimensions={1,2}, to_apply=%bitcast.79.reduce_sub_computation | reduce | bytes 819202
  81.3 136.3 %all_to_all.84 = bf16[16,2,6400]{2,1,0:T(2,128)(2,1)} all-to-all(bf16[16,2,6400]{2,1,0:T(2,128)(2,1)S(1)} %reshape.191), channel_id=1, replica_groups=mesh['dp'=16,'tensor'=16] {'tensor'}, dimensions={0} | all-to-all | bytes 819200 | tf_op jit(solution)/shard_map/all_to_all | solution.py:28
  217.6 2.7 reshape.192
  220.3 7.6 %bitcast_reduce_fusion = bf16[128,1600]{0,1:T(8,128)(2,1)} fusion(bf16[1600,1,1,128]{3,2,1,0:T(2,128)(2,1)S(1)} %reshape.192), kind=kLoop, calls=%fused_computation.59 | loop fusion | bytes 819200 | tf_op jit(solution)/shard_map/all_to_all | solution.py:28
  230.4 10.6 %all-to-all-start.4 = ((bf16[16,128,1,100]{1,3,2,0:T(8,128)(2,1)}), bf16[16,128,1,100]{1,3,2,0:T(8,128)(2,1)}, u32[]{:S(2)}, u32[]{:S(2)}) async-start(bf16[16,128,1,100]{1,3,2,0:T(8,128)(2,1)} %copy.32), calls=%async_computation.5 | async-start | bytes 851968 | tf_op jit(solution)/shard_map/all_to_all | solution.py:35
  242.2 6.4 %copy.53 = bf16[1,128,1,1600]{1,2,0,3:T(2,128)(2,1)S(1)} copy(bf16[1,128,1,1600]{1,3,2,0:T(8,128)(2,1)S(1)} %convert_bitcast_fusion) | data formatting | bytes 819200 | tf_op jit(solution)/shard_map/reshape | solution.py:25
  248.6 9.9 %reduce.4 = bf16[1600,128]{1,0:T(8,128)(2,1)} reduce(bf16[1600,1,1,128]{3,2,1,0:T(2,128)(2,1)S(1)} %bitcast.84, bf16[]{:T(256)} %broadcast.410), dimensions={1,2}, to_apply=%bitcast.80.reduce_sub_computation | reduce | bytes 819202
  260.4 9.7 %all-to-all-start.1 = ((bf16[16,2,6400]{2,1,0:T(2,128)(2,1)}), bf16[16,2,6400]{2,1,0:T(2,128)(2,1)S(1)}, u32[]{:S(2)}, u32[]{:S(2)}) async-start(bf16[16,2,6400]{2,1,0:T(2,128)(2,1)} %reshape.189), calls=%async_computation.2 | async-start | bytes 819200 | tf_op jit(solution)/shard_map/all_to_all | solution.py:28
  271.1 7.4 %all-to-all-done.1 = bf16[16,2,6400]{2,1,0:T(2,128)(2,1)S(1)} async-done(((bf16[16,2,6400]{2,1,0:T(2,128)(2,1)}), bf16[16,2,6400]{2,1,0:T(2,128)(2,1)S(1)}, u32[]{:S(2)}, u32[]{:S(2)}) %all-to-all-start.1) | async-done | bytes 409632 | tf_op jit(solution)/shard_map/all_to_all | solution.py:28
  278.5 4.0 stack.3
  282.5 5.2 %all-to-all-start.5 = ((bf16[16,128,1600]{1,2,0:T(8,128)(2,1)}), bf16[16,128,1600]{1,2,0:T(8,128)(2,1)}, u32[]{:S(2)}, u32[]{:S(2)}) async-start(bf16[16,128,1600]{1,2,0:T(8,128)(2,1)} %stack.3), calls=%async_computation.6 | async-start | bytes 13107200 | tf_op jit(solution)/shard_map/all_to_all | solution.py:60
  287.7 2.7 reshape.190
  290.4 7.6 %bitcast_reduce_fusion.1 = bf16[128,1600]{0,1:T(8,128)(2,1)} fusion(bf16[1600,1,1,128]{3,2,1,0:T(2,128)(2,1)S(1)} %reshape.190), kind=kLoop, calls=%fused_computation.60 | loop fusion | bytes 819200 | tf_op jit(solution)/shard_map/all_to_all | solution.py:28
  300.5 135.2 %all-to-all-done.5 = bf16[16,128,1600]{1,2,0:T(8,128)(2,1)} async-done(((bf16[16,128,1600]{1,2,0:T(8,128)(2,1)}), bf16[16,128,1600]{1,2,0:T(8,128)(2,1)}, u32[]{:S(2)}, u32[]{:S(2)}) %all-to-all-start.5) | async-done | bytes 6553632 | tf_op jit(solution)/shard_map/all_to_all | solution.py:60
  435.6 8.9 %all-to-all-start.2 = ((bf16[16,128,1,100]{1,3,2,0:T(8,128)(2,1)}), bf16[16,128,1,100]{1,3,2,0:T(8,128)(2,1)S(1)}, u32[]{:S(2)}, u32[]{:S(2)}) async-start(bf16[16,128,1,100]{1,3,2,0:T(8,128)(2,1)} %copy.29), calls=%async_computation.3 | async-start | bytes 851968 | tf_op jit(solution)/shard_map/all_to_all | solution.py:35
  444.5 7.1 %convolution_bitcast_fusion.1 = f32[320,1600]{1,0:T(8,128)} fusion(bf16[16,128,1600]{1,2,0:T(8,128)(2,1)} %all-to-all-done.5, bf16[128,16,320]{0,2,1:T(8,128)(2,1)} %all-to-all-done), kind=kOutput, calls=%fused_computation.1 | convolution fusion | flops 2097152000 | bytes 9912320 | tf_op jit(solution)/shard_map/dot_general | solution.py:57
  451.7 3.1 copy.33
  457.8 5.3 %fusion.19 = (bf16[128,1600]{0,1:T(8,128)(2,1)}, bf16[128,1600]{0,1:T(8,128)(2,1)}) fusion(bf16[128,1600]{0,1:T(8,128)(2,1)} %param.8, bf16[128,1600]{0,1:T(8,128)(2,1)} %param.9, bf16[1600,1600]{1,0:T(8,128)(2,1)} %param.13, bf16[128,1600]{0,1:T(8,128)(2,1)S(1)} %reshape.180), kind=kOutput, calls=%fused_computation.33 | convolution fusion | flops 658432000 | bytes 7168000 | tf_op jit(solution)/shard_map/dot_general | solution.py:75
  (31 shorter events, 18.5 us)
Async XLA Ops:
  9.6 37.6 %all-to-all-start = ((bf16[128,16,320]{0,2,1:T(8,128)(2,1)}), bf16[128,16,320]{0,2,1:T(8,128)(2,1)}, u32[]{:S(2)}, u32[]{:S(2)}) async-start(bf16[128,16,320]{0,2,1:T(8,128)(2,1)} %bitcast.4), calls=%async_computation | async-start | bytes 2621440 | tf_op jit(solution)/shard_map/all_to_all | solution.py:56
  16.2 2.4 copy-start.1
  16.2 2.4 copy-start.2
  16.2 224.8 %reduce-scatter.2.cloned.1.call-start = ((), (), s32[]{:S(2)}) async-start(), calls=%async_computation.7 | async-start | bytes 13926400 | tf_op jit(solution)/shard_map/reduce_scatter | solution.py:68
  57.1 1.0 copy-start.3
  57.1 1.1 copy-start.4
  230.4 30.0 %all-to-all-start.4 = ((bf16[16,128,1,100]{1,3,2,0:T(8,128)(2,1)}), bf16[16,128,1,100]{1,3,2,0:T(8,128)(2,1)}, u32[]{:S(2)}, u32[]{:S(2)}) async-start(bf16[16,128,1,100]{1,3,2,0:T(8,128)(2,1)} %copy.32), calls=%async_computation.5 | async-start | bytes 851968 | tf_op jit(solution)/shard_map/all_to_all | solution.py:35
  260.4 18.2 %all-to-all-start.1 = ((bf16[16,2,6400]{2,1,0:T(2,128)(2,1)}), bf16[16,2,6400]{2,1,0:T(2,128)(2,1)S(1)}, u32[]{:S(2)}, u32[]{:S(2)}) async-start(bf16[16,2,6400]{2,1,0:T(2,128)(2,1)} %reshape.189), calls=%async_computation.2 | async-start | bytes 819200 | tf_op jit(solution)/shard_map/all_to_all | solution.py:28
  278.5 4.0 copy-start
  282.5 153.1 %all-to-all-start.5 = ((bf16[16,128,1600]{1,2,0:T(8,128)(2,1)}), bf16[16,128,1600]{1,2,0:T(8,128)(2,1)}, u32[]{:S(2)}, u32[]{:S(2)}) async-start(bf16[16,128,1600]{1,2,0:T(8,128)(2,1)} %stack.3), calls=%async_computation.6 | async-start | bytes 13107200 | tf_op jit(solution)/shard_map/all_to_all | solution.py:60
  435.6 22.1 %all-to-all-start.2 = ((bf16[16,128,1,100]{1,3,2,0:T(8,128)(2,1)}), bf16[16,128,1,100]{1,3,2,0:T(8,128)(2,1)S(1)}, u32[]{:S(2)}, u32[]{:S(2)}) async-start(bf16[16,128,1,100]{1,3,2,0:T(8,128)(2,1)} %copy.29), calls=%async_computation.3 | async-start | bytes 851968 | tf_op jit(solution)/shard_map/all_to_all | solution.py:35
Sparse Core Ops, SparseCore 0:
  57.2 165.9 reduce-scatter.1
